TPU v7x, 256 devices: a whole 4x4x8 slice. The times are simulated.
256 devices in a mesh: tensor: 4 (over z_lo, core), request: 64 (over x, y, z_hi).
Axes of the slice: x: 4, y: 4, z: 8 (z_hi: 4, z_lo: 2; z = z_hi * 2 + z_lo), core: 2. Of those that a mesh axis runs over, the one named last changes fastest.
Arguments:
- hidden_in: bfloat16 [16384, 2048], P('request'), may hold values from -6 to 6
- span_q: bfloat16 [16384, 2048], P('request', 'tensor'), may hold values from -170 to 170
- span_k: bfloat16 [16384, 2048], P('request', 'tensor'), may hold values from -7 to 7
- span_v: bfloat16 [16384, 2048], P('request', 'tensor'), may hold values from -6 to 6
- cache_k: bfloat16 [64, 768, 2048], P('request', None, 'tensor'), may hold values from -6 to 6
- cache_v: bfloat16 [64, 768, 2048], P('request', None, 'tensor'), may hold values from -6 to 6
- cached_len: int32 [64], P('request'), may hold values from 0 to 768
- out_proj: bfloat16 [2048, 2048], P('tensor'), may hold values from -0.125 to 0.125
- norm_gain: float32 [2048], replicated, may hold values from 0.1 to 1.9
- routes: int32 [16384, 4], P('request'), may hold values from 0 to 63, all different within a row; in each aligned block of 256 rows (0 to 255, 256 to 511, ...) at most 32 rows name the same one
- route_weight: float32 [16384, 4], P('request'), may hold values from 0.1 to 1
- w_gate: bfloat16 [64, 2048, 1408], P('request', None, 'tensor'), may hold values from -0.125 to 0.125
- w_up: bfloat16 [64, 2048, 1408], P('request', None, 'tensor'), may hold values from -0.125 to 0.125
- w_down: bfloat16 [64, 1408, 2048], P('request', 'tensor'), may hold values from -0.15625 to 0.15625
Outputs:
- layer_out: bfloat16 [16384, 2048], P('request', 'tensor')
- decode_kv: bfloat16 [64, 2, 1024, 2048], P('request', None, 'tensor')
Inputs may be any that keep to these rules, and one draw needn't show every extreme that they name: `routes`: among the rows of one request no expert is named more than 32 times.
All inputs are finite; a program needn't handle non-finite values.
Results may differ from a plain program's by a relative error of at most 0.014.
Values may be sent and summed in bfloat16 or wider, within the bound.
No kernel may reach another device: no remote copies, remote signals or barrier semaphores. Data moves between devices by JAX's collectives and lax.ppermute only.
A program may use at most 128 MiB of HBM per device.

v0:
```python
import jax
import jax.numpy as jnp
from jax import lax
from jax.sharding import PartitionSpec as P

HD = 128
TOP = 4


eps = 1e-06
neg_large = -1e30


def attend(span_q, span_k, span_v, cache_k, cache_v, length):
    span = span_q.shape[0]
    prior = cache_k.shape[1]
    heads = span_q.shape[1] // HD
    keys = jnp.concatenate([cache_k[0], span_k], axis=0).reshape(prior + span, heads, HD)
    values = jnp.concatenate([cache_v[0], span_v], axis=0).reshape(prior + span, heads, HD)
    query = span_q.reshape(span, heads, HD)
    scores = jnp.einsum("qhd,khd->hqk", query, keys, preferred_element_type=jnp.float32) * HD ** (
        -0.5
    )
    key_pos = jnp.arange(prior + span, dtype=jnp.int32)[None, :]
    row_pos = jnp.arange(span, dtype=jnp.int32)[:, None]
    valid = jnp.where(key_pos < prior, key_pos < length, key_pos - prior <= row_pos)
    scores = jnp.where(valid[None], scores, neg_large)
    top = jnp.max(scores, axis=2, keepdims=True)
    weights = jnp.exp(scores - top)
    probs = (weights / jnp.sum(weights, axis=2, keepdims=True)).astype(jnp.bfloat16)
    attended = jnp.einsum("hqk,khd->qhd", probs, values, preferred_element_type=jnp.float32)
    return attended.astype(jnp.bfloat16).reshape(span, heads * HD)


def place(cached, fresh, length, context):
    span = fresh.shape[0]
    positions = jnp.arange(context, dtype=jnp.int32)
    padded = jnp.concatenate([cached[0], jnp.zeros((span, cached.shape[2]), cached.dtype)], axis=0)
    kept = jnp.where((positions < length)[:, None], padded, jnp.zeros_like(padded))
    return lax.dynamic_update_slice(kept, fresh, (length, jnp.int32(0)))


def on_device(
    hidden_in,
    span_q,
    span_k,
    span_v,
    cache_k,
    cache_v,
    cached_len,
    out_proj,
    norm_gain,
    routes,
    route_weight,
    w_gate,
    w_up,
    w_down,
):
    span, width = hidden_in.shape
    groups = lax.axis_size("tensor")
    quarter = width // groups
    offset = lax.axis_index("tensor") * quarter
    length = cached_len[0]
    attended = attend(span_q, span_k, span_v, cache_k, cache_v, length)
    attn_part = jnp.dot(attended, out_proj, preferred_element_type=jnp.float32)
    attn_full = lax.psum(attn_part.astype(jnp.bfloat16), "tensor").astype(jnp.float32)
    mixed = (hidden_in.astype(jnp.float32) + attn_full).astype(jnp.bfloat16)
    mixed_f = mixed.astype(jnp.float32)
    normed = (
        mixed_f * lax.rsqrt(jnp.mean(mixed_f * mixed_f, axis=1, keepdims=True) + eps) * norm_gain
    ).astype(jnp.bfloat16)
    own_mixed = lax.dynamic_slice_in_dim(mixed, offset, quarter, 1)
    experts = lax.axis_size("request")
    most = max(2, 2 * span * TOP // experts)
    flat = routes.reshape(-1)
    onehot = (flat[:, None] == jnp.arange(experts, dtype=jnp.int32)[None, :]).astype(jnp.int32)
    before = jnp.cumsum(onehot, axis=0) - onehot
    slot = jnp.sum(before * onehot, axis=1)
    dest = flat * most + slot
    source_row = jnp.arange(span * TOP, dtype=jnp.int32) // TOP
    outbox = (
        jnp.zeros((experts * most, normed.shape[1]), jnp.bfloat16).at[dest].set(normed[source_row])
    )
    inbox = lax.all_to_all(outbox, "request", split_axis=0, concat_axis=0, tiled=True)
    gate_w = w_gate[0]
    up_w = w_up[0]
    down_w = w_down[0]
    gate = jnp.dot(inbox, gate_w, preferred_element_type=jnp.float32)
    upper = jnp.dot(inbox, up_w, preferred_element_type=jnp.float32)
    act = (jax.nn.silu(gate) * upper).astype(jnp.bfloat16)
    partial_out = jnp.dot(act, down_w, preferred_element_type=jnp.float32)
    shares = lax.psum_scatter(
        partial_out.astype(jnp.bfloat16), "tensor", scatter_dimension=1, tiled=True
    )
    returned = lax.all_to_all(shares, "request", split_axis=0, concat_axis=0, tiled=True)
    picked = returned[dest].reshape(span, TOP, quarter).astype(jnp.float32)
    mixture = jnp.sum(picked * route_weight[:, :, None], axis=1)
    layer_out = (own_mixed.astype(jnp.float32) + mixture).astype(jnp.bfloat16)
    context = cache_k.shape[1] + span
    local = jnp.stack(
        [place(cache_k, span_k, length, context), place(cache_v, span_v, length, context)], axis=0
    )[None]
    decode_kv = lax.all_to_all(local, "tensor", split_axis=2, concat_axis=3, tiled=True)
    return (layer_out, decode_kv)


def solution(mesh):
    in_specs = (
        P("request", None),
        P("request", "tensor"),
        P("request", "tensor"),
        P("request", "tensor"),
        P("request", None, "tensor"),
        P("request", None, "tensor"),
        P("request"),
        P("tensor", None),
        P(),
        P("request", None),
        P("request", None),
        P("request", None, "tensor"),
        P("request", None, "tensor"),
        P("request", "tensor", None),
    )
    out_specs = (P("request", "tensor"), P("request", None, "tensor", None))
    return jax.shard_map(
        on_device, mesh=mesh, in_specs=in_specs, out_specs=out_specs, check_vma=False
    )
```

profile of v0, /device:TPU:32, one launch (start us, length us, event | category | flops | bytes accessed | tf_op | source)
XLA Modules:
  0.0 500.7 jit_solution(1071059432460148645)
XLA Ops:
  8.1 1.4 copy.55
  9.5 1.2 copy.57
  11.5 1.8 copy.58
  13.3 2.3 copy.53
  16.5 0.9 fusion.25
  17.3 1.7 fusion.21
  19.1 2.1 fusion.36
  21.8 1.7 convolution_convert_fusion.1
  24.0 18.0 %reduce-window.6 = s32[64,8,128]{2,1,0:T(8,128)S(1)} reduce-window(s32[64,8,128]{2,1,0:T(8,128)S(1)} %fusion.31, s32[]{:T(128)} %constant.51.clone.1), window={size=1x1x128 pad=0_0x0_0x127_0}, to_apply=%region_3.4 | reduce-window | flops 8323072 | bytes 524292 | tf_op jit(solution)/shard_map/reduce-window
  42.9 28.9 %all-reduce.4.cloned.1.call-done = bf16[256,2048]{1,0:T(8,128)(2,1)} async-done(((bf16[256,2048]{1,0:T(8,128)(2,1)}), bf16[256,2048]{1,0:T(8,128)(2,1)}) %all-reduce.4.cloned.1.call-update) | async-done | bytes 1048592 | tf_op jit(solution)/shard_map/psum | solution.py:66
  71.9 1.7 fusion.6
  74.0 25.3 %scatter_custom_fusion = bf16[2048,2048]{1,0:T(8,128)(2,1)} fusion(s32[1024]{0:T(1024)S(1)} %bitcast.99, bf16[256,2048]{1,0:T(8,128)(2,1)S(1)} %fusion.8, s32[1024]{0:T(1024)S(1)} %broadcast_clamp_fusion.1, bf16[]{:T(256)} %constant.56.clone.1), kind=kCustom, calls=%fused_computation.6 | custom fusion | bytes 8388610 | tf_op jit(solution)/shard_map/scatter | solution.py:82
  99.3 202.0 %all_to_all.42 = bf16[64,32,2048]{2,1,0:T(8,128)(2,1)S(1)} all-to-all(bf16[64,32,2048]{2,1,0:T(8,128)(2,1)} %bitcast.82), channel_id=1, replica_groups=mesh['tensor'=4,'request'=64] {'request'}, dimensions={0} | all-to-all | bytes 16777216 | tf_op jit(solution)/shard_map/all_to_all | solution.py:84
  301.4 3.2 fusion.15
  304.6 3.5 fusion.5
  308.1 6.8 %convolution_convert_fusion = bf16[2048,2048]{1,0:T(8,128)(2,1)} fusion(bf16[2048,352]{0,1:T(8,128)(2,1)S(1)} %fusion.5, bf16[1,352,2048]{2,1,0:T(8,128)(2,1)S(1)} %copy-done.16), kind=kOutput, calls=%fused_computation.4 | convolution fusion | flops 2956984320 | bytes 11272192 | tf_op jit(solution)/shard_map/dot_general | solution.py:91
  315.0 1.1 copy-done.3
  316.1 2.5 select_bitcast_fusion.1
  318.6 1.8 dynamic_update_slice.8
  320.4 1.0 copy-done.2
  321.4 2.8 dynamic_update_slice.9
  324.2 1.8 maximum_bitcast_fusion
  325.9 2.2 copy.67
  328.1 50.8 %all_to_all.43 = bf16[1,2,1024,512]{3,1,0,2:T(2,128)(2,1)S(1)} all-to-all(bf16[1,2,1024,512]{3,1,0,2:T(2,128)(2,1)S(1)} %copy.67), channel_id=1, replica_groups=mesh['tensor'=4,'request'=64] {'tensor'}, dimensions={2} | all-to-all | bytes 4194304 | tf_op jit(solution)/shard_map/all_to_all | solution.py:103
  378.9 32.7 %reduce-scatter.2.cloned.1.call-done = bf16[2048,512]{1,0:T(8,128)(2,1)} async-done(((bf16[2048,2048]{1,0:T(8,128)(2,1)}), bf16[2048,512]{1,0:T(8,128)(2,1)}) %reduce-scatter.2.cloned.1.call-update) | async-done | bytes 2097168 | tf_op jit(solution)/shard_map/reduce_scatter | solution.py:92
  411.6 13.8 %all-to-all-start.1 = ((bf16[64,32,512]{2,1,0:T(8,128)(2,1)}), bf16[64,32,512]{2,1,0:T(8,128)(2,1)}, u32[]{:S(2)}, u32[]{:S(2)}) async-start(bf16[64,32,512]{2,1,0:T(8,128)(2,1)} %bitcast.89), calls=%async_computation.2 | async-start | bytes 4194304 | tf_op jit(solution)/shard_map/all_to_all | solution.py:95
  425.6 2.9 copy.68
  428.5 4.4 all_to_all.38
  432.9 47.1 %all-to-all-done.1 = bf16[64,32,512]{2,1,0:T(8,128)(2,1)} async-done(((bf16[64,32,512]{2,1,0:T(8,128)(2,1)}), bf16[64,32,512]{2,1,0:T(8,128)(2,1)}, u32[]{:S(2)}, u32[]{:S(2)}) %all-to-all-start.1) | async-done | bytes 2097184 | tf_op jit(solution)/shard_map/all_to_all | solution.py:95
  480.0 7.2 %gather_fusion = bf16[1024,512]{1,0:T(8,128)(2,1)} fusion(bf16[2048,512]{1,0:T(8,128)(2,1)} %bitcast.19, s32[1024]{0:T(1024)S(1)} %broadcast_clamp_fusion), kind=kCustom, calls=%fused_computation.1 | custom fusion | bytes 2101248 | tf_op jit(solution)/shard_map/gather | solution.py:96
  487.2 2.7 reshape.201
  489.9 2.9 multiply_reduce_fusion
  (63 shorter events, 4.9 us)
Async XLA Ops:
  7.2 14.6 %copy-start = (bf16[512,2048]{1,0:T(8,128)(2,1)S(1)}, bf16[512,2048]{1,0:T(8,128)(2,1)}, u32[]{:S(2)}) copy-start(bf16[512,2048]{1,0:T(8,128)(2,1)} %param.21) | copy-start | bytes 6291460
  7.2 3.5 copy-start.5
  7.2 64.7 %all-reduce.4.cloned.1.call-start = ((), (), s32[]{:S(2)}) async-start(), calls=%async_computation.4 | async-start | bytes 2097152 | tf_op jit(solution)/shard_map/psum | solution.py:66
  8.1 7.6 %copy-start.6 = (bf16[256,512]{1,0:T(8,128)(2,1)S(1)}, bf16[256,512]{1,0:T(8,128)(2,1)}, u32[]{:S(2)}) copy-start(bf16[256,512]{1,0:T(8,128)(2,1)} %param.17) | copy-start | bytes 786436
  10.7 6.6 %copy-start.4 = (bf16[768,4,128]{2,0,1:T(8,128)(2,1)S(1)}, bf16[768,4,128]{2,0,1:T(8,128)(2,1)}, u32[]{:S(2)}) copy-start(bf16[768,4,128]{2,0,1:T(8,128)(2,1)} %copy.57) | copy-start | bytes 2359300
  19.1 2.2 copy-start.9
  19.1 2.2 copy-start.10
  21.7 1.8 copy-start.11
  23.5 48.4 %copy-start.8 = (bf16[256,2048]{1,0:T(8,128)(2,1)S(1)}, bf16[256,2048]{1,0:T(8,128)(2,1)}, u32[]{:S(2)}) copy-start(bf16[256,2048]{1,0:T(8,128)(2,1)} %param.14) | copy-start | bytes 3145732
  23.5 388.1 %reduce-scatter.2.cloned.1.call-start = ((), (), s32[]{:S(2)}) async-start(), calls=%async_computation.5 | async-start | bytes 10485760 | tf_op jit(solution)/shard_map/reduce_scatter | solution.py:92
  24.0 49.7 %copy-start.12 = (f32[2048]{0:T(1024)S(1)}, f32[2048]{0:T(1024)}, u32[]{:S(2)}) copy-start(f32[2048]{0:T(1024)} %param.22) | copy-start | bytes 24580
  99.3 202.1 %copy-start.14 = (bf16[1,2048,352]{1,2,0:T(8,128)(2,1)S(1)}, bf16[1,2048,352]{1,2,0:T(8,128)(2,1)}, u32[]{:S(2)}) copy-start(bf16[1,2048,352]{1,2,0:T(8,128)(2,1)} %param.25) | copy-start | bytes 4325380
  301.4 3.2 copy-start.15
  304.6 3.5 copy-start.16
  315.0 1.1 copy-start.3
  315.0 6.4 %copy-start.7 = (bf16[256,512]{1,0:T(8,128)(2,1)S(1)}, bf16[256,512]{1,0:T(8,128)(2,1)}, u32[]{:S(2)}) copy-start(bf16[256,512]{1,0:T(8,128)(2,1)} %param.17) | copy-start | bytes 786436
  320.4 1.0 copy-start.2
  378.9 46.5 %copy-start.13 = (f32[256,4]{0,1:T(4,128)S(1)}, f32[256,4]{0,1:T(4,128)}, u32[]{:S(2)}) copy-start(f32[256,4]{0,1:T(4,128)} %param.24) | copy-start | bytes 12292
  411.6 68.4 %all-to-all-start.1 = ((bf16[64,32,512]{2,1,0:T(8,128)(2,1)}), bf16[64,32,512]{2,1,0:T(8,128)(2,1)}, u32[]{:S(2)}, u32[]{:S(2)}) async-start(bf16[64,32,512]{2,1,0:T(8,128)(2,1)} %bitcast.89), calls=%async_computation.2 | async-start | bytes 4194304 | tf_op jit(solution)/shard_map/all_to_all | solution.py:95
  480.0 13.7 %copy-start.1 = (bf16[512,2048]{1,0:T(8,128)(2,1)S(1)}, bf16[512,2048]{1,0:T(8,128)(2,1)}, u32[]{:S(2)}) copy-start(bf16[512,2048]{1,0:T(8,128)(2,1)} %param.21) | copy-start | bytes 6291460
Sparse Core Ops, SparseCore 0:
  23.6 48.2 all-reduce.3
  315.1 96.4 reduce-scatter.1
where the time goes:
time: 507 us; the launch traced here: 501 us
  blocking collectives  253 us (50%)
  waiting for transfers between devices  109 us (21%)
  local copies, waits for them, and re-layouts  61 us (12%)
  other arithmetic  31.3 us (6%)
  matrix products  17.5 us (3%)
  between operations  15.5 us (3%)
  starting transfers between devices  13.8 us (3%)
    all_to_all x1, blocking collectives, on_device(): lax.all_to_all(outbox, 'request', split_axis=0, concat_axis=0, tiled=True)  202 us
    all_to_all x1, blocking collectives, on_device(): lax.all_to_all(local, 'tensor', split_axis=2, concat_axis=3, tiled=True)  50.8 us
    all_to_all x1, waiting for transfers between devices, on_device(): lax.all_to_all(shares, 'request', split_axis=0, concat_axis=0, tiled=True)  47.1 us
    reduce_scatter x1, waiting for transfers between devices, on_device(): lax.psum_scatter(partial_out.astype(jnp.bfloat16), 'tensor', scatter_dime...  32.7 us
    psum x1, waiting for transfers between devices, on_device(): lax.psum(attn_part.astype(jnp.bfloat16), 'tensor').astype(jnp.float32)  28.9 us
    scatter x1, local copies, waits for them, and re-layouts, on_device(): jnp.zeros((experts * most, normed.shape[1]), jnp.bfloat16).at[dest]  25.3 us
    another operation x3, other arithmetic  18.2 us
    all_to_all x1, starting transfers between devices, on_device(): lax.all_to_all(shares, 'request', split_axis=0, concat_axis=0, tiled=True)  13.8 us
  transfers between devices with their start and end apart: 3, of which 3 were waited for; matrix products, arithmetic and copies ran while one was open for 7% of the time, Pallas kernels for 0%

commit v1 on v0

v1 whole, which is shorter than its diff:
```python
import jax
import jax.numpy as jnp
from jax import lax
from jax.sharding import PartitionSpec as P


HD = 128
TOP = 4


eps = 1e-06
neg_large = -1e30


def attend(span_q, span_k, span_v, cache_k, cache_v, length):
    span = span_q.shape[0]
    prior = cache_k.shape[1]
    heads = span_q.shape[1] // HD
    keys = jnp.concatenate([cache_k[0], span_k], axis=0).reshape(prior + span, heads, HD)
    values = jnp.concatenate([cache_v[0], span_v], axis=0).reshape(prior + span, heads, HD)
    query = span_q.reshape(span, heads, HD)
    scores = lax.dot_general(
        query, keys, (((2,), (2,)), ((1,), (1,))), preferred_element_type=jnp.float32
    )
    scores = scores * HD ** (-0.5)
    key_pos = jnp.arange(prior + span, dtype=jnp.int32)[None, :]
    row_pos = jnp.arange(span, dtype=jnp.int32)[:, None]
    valid = jnp.where(key_pos < prior, key_pos < length, key_pos - prior <= row_pos)
    scores = jnp.where(valid[None], scores, neg_large)
    top = jnp.max(scores, axis=2, keepdims=True)
    weights = jnp.exp(scores - top)
    probs = (weights / jnp.sum(weights, axis=2, keepdims=True)).astype(jnp.bfloat16)
    attended = jnp.einsum("hqk,khd->qhd", probs, values, preferred_element_type=jnp.float32)
    return attended.astype(jnp.bfloat16).reshape(span, heads * HD)


def place(cached, fresh, length, context):
    span = fresh.shape[0]
    positions = jnp.arange(context, dtype=jnp.int32)
    padded = jnp.concatenate([cached[0], jnp.zeros((span, cached.shape[2]), cached.dtype)], axis=0)
    kept = jnp.where((positions < length)[:, None], padded, jnp.zeros_like(padded))
    return lax.dynamic_update_slice(kept, fresh, (length, jnp.int32(0)))


def flip(value, mask):
    groups = lax.axis_size("tensor")
    return lax.ppermute(value, "tensor", [(i, i ^ mask) for i in range(groups)])


def on_device(
    hidden_in,
    span_q,
    span_k,
    span_v,
    cache_k,
    cache_v,
    cached_len,
    out_proj,
    norm_gain,
    routes,
    route_weight,
    w_gate,
    w_up,
    w_down,
):
    span, width = hidden_in.shape
    groups = lax.axis_size("tensor")
    experts = lax.axis_size("request")
    quarter = width // groups
    half = width // 2
    me = lax.axis_index("tensor")
    core = me % 2
    length = cached_len[0]

    own_w = (w_gate[0], w_up[0], w_down[0])
    far_w, near_w, diag_w = [], [], []
    for shard in own_w:
        far_w.append(flip(shard, 2))
        near_w.append(flip(shard, 1))
        diag_w.append(flip(far_w[-1], 1))

    most = max(2, 2 * span * TOP // experts)
    share = most // groups
    expert_ids = jnp.arange(experts, dtype=jnp.int32)
    hit = routes[:, :, None] == expert_ids[None, None, :]
    member = jnp.any(hit, axis=1)
    weight_of = jnp.sum(jnp.where(hit, route_weight[:, :, None], 0.0), axis=1)
    lower = jnp.arange(span)[:, None] > jnp.arange(span)[None, :]
    rank = jnp.dot(
        lower.astype(jnp.bfloat16), member.astype(jnp.bfloat16), preferred_element_type=jnp.float32
    ).astype(jnp.int32)
    slot = jnp.where(member, rank - me * share, -1)
    chosen = slot[:, :, None] == jnp.arange(share, dtype=jnp.int32)[None, None, :]
    select = chosen.reshape(span, experts * share).astype(jnp.bfloat16)
    w_hi = lax.reduce_precision(weight_of, 8, 7)
    w_lo = weight_of - w_hi
    mix_hi = jnp.where(chosen, w_hi[:, :, None], 0.0).reshape(span, experts * share)
    mix_lo = jnp.where(chosen, w_lo[:, :, None], 0.0).reshape(span, experts * share)
    mix_hi = mix_hi.astype(jnp.bfloat16)
    mix_lo = mix_lo.astype(jnp.bfloat16)

    attended = attend(span_q, span_k, span_v, cache_k, cache_v, length)
    part = jnp.dot(attended, out_proj, preferred_element_type=jnp.float32)
    chip = part + flip(part.astype(jnp.bfloat16), 1).astype(jnp.float32)
    chip_half = lax.dynamic_slice_in_dim(chip, core * half, half, 1)
    full_half = chip_half + flip(chip_half.astype(jnp.bfloat16), 2).astype(jnp.float32)
    hidden_half = lax.dynamic_slice_in_dim(hidden_in, core * half, half, 1)
    mixed_half = (hidden_half.astype(jnp.float32) + full_half).astype(jnp.bfloat16)
    other_half = flip(mixed_half, 1)
    first = core == 0
    mixed = jnp.concatenate(
        [jnp.where(first, mixed_half, other_half), jnp.where(first, other_half, mixed_half)], axis=1
    )
    mixed_f = mixed.astype(jnp.float32)
    normed = (
        mixed_f * lax.rsqrt(jnp.mean(mixed_f * mixed_f, axis=1, keepdims=True) + eps) * norm_gain
    ).astype(jnp.bfloat16)
    own_mixed = lax.dynamic_slice_in_dim(mixed, me * quarter, quarter, 1)

    outbox = lax.dot_general(
        select, normed, (((0,), (0,)), ((), ())), preferred_element_type=jnp.float32
    ).astype(jnp.bfloat16)
    inbox = lax.all_to_all(outbox, "request", split_axis=0, concat_axis=0, tiled=True)

    context = cache_k.shape[1] + span
    local = jnp.stack(
        [place(cache_k, span_k, length, context), place(cache_v, span_v, length, context)], axis=0
    )
    local, inbox = lax.optimization_barrier((local, inbox))

    total = jnp.zeros((inbox.shape[0], width), jnp.float32)
    for gate_w, up_w, down_w in (own_w, near_w, far_w, diag_w):
        gate = jnp.dot(inbox, gate_w, preferred_element_type=jnp.float32)
        upper = jnp.dot(inbox, up_w, preferred_element_type=jnp.float32)
        act = (jax.nn.silu(gate) * upper).astype(jnp.bfloat16)
        total = total + jnp.dot(act, down_w, preferred_element_type=jnp.float32)
    expert_out = total.astype(jnp.bfloat16)

    block = context // groups
    decode = jnp.zeros((2, block, width), jnp.bfloat16)
    for mask in range(groups):
        peer = me ^ mask
        piece = lax.dynamic_slice_in_dim(local, peer * block, block, 1)
        if mask:
            piece = flip(piece, mask)
        decode = lax.dynamic_update_slice_in_dim(decode, piece, peer * quarter, 2)

    returned = lax.all_to_all(expert_out, "request", split_axis=0, concat_axis=0, tiled=True)
    mixture = jnp.dot(mix_hi, returned, preferred_element_type=jnp.float32) + jnp.dot(
        mix_lo, returned, preferred_element_type=jnp.float32
    )
    result = own_mixed.astype(jnp.float32) + lax.dynamic_slice_in_dim(
        mixture, me * quarter, quarter, 1
    )
    for mask in range(1, groups):
        piece = lax.dynamic_slice_in_dim(mixture, (me ^ mask) * quarter, quarter, 1)
        result = result + flip(piece.astype(jnp.bfloat16), mask).astype(jnp.float32)
    layer_out = result.astype(jnp.bfloat16)
    return (layer_out, decode[None])


def solution(mesh):
    in_specs = (
        P("request", None),
        P("request", "tensor"),
        P("request", "tensor"),
        P("request", "tensor"),
        P("request", None, "tensor"),
        P("request", None, "tensor"),
        P("request"),
        P("tensor", None),
        P(),
        P("request", None),
        P("request", None),
        P("request", None, "tensor"),
        P("request", None, "tensor"),
        P("request", "tensor", None),
    )
    out_specs = (P("request", "tensor"), P("request", None, "tensor", None))

    return jax.shard_map(
        on_device, mesh=mesh, in_specs=in_specs, out_specs=out_specs, check_vma=False
    )
```

time: 507 us -> 321 us (0.63)
  blocking collectives: 253 us -> 0 us
  waiting for transfers between devices: 109 us -> 189 us
  local copies, waits for them, and re-layouts: 61 us -> 23.9 us
  matrix products: 17.5 us -> 52.5 us
  starting transfers between devices: 13.8 us -> 35.7 us
  other arithmetic: 31.3 us -> 14.8 us
  between operations: 15.5 us -> 1.77 us
    all_to_all x2 -> x0, blocking collectives: 253 us -> none  [the longest x1 202 us: on_device(): lax.all_to_all(outbox, 'request', split_axis=0, concat_axis=0, tiled=True)]
    ppermute x0 -> x18, waiting for transfers between devices: none -> 142 us  [flip(): return lax.ppermute(value, 'tensor', [(i, i ^ mask) for i in range(groups)])]
    reduce_scatter x1 -> x0, waiting for transfers between devices: 32.7 us -> none  [on_device(): lax.psum_scatter(partial_out.astype(jnp.bfloat16), 'tensor', scatter_dime...]
    psum x1 -> x0, waiting for transfers between devices: 28.9 us -> none  [on_device(): lax.psum(attn_part.astype(jnp.bfloat16), 'tensor').astype(jnp.float32)]
    dot_general x4 -> x10, matrix products: 13.8 us -> 39.3 us  [the longest x4 28 us: on_device(): total = total + jnp.dot(act, down_w, preferred_element_type=jnp.float32)]
    scatter x1 -> x0, local copies, waits for them, and re-layouts: 25.3 us -> none  [on_device(): jnp.zeros((experts * most, normed.shape[1]), jnp.bfloat16).at[dest]]
    another operation x3 -> x0, other arithmetic: 18.2 us -> none
    all_to_all x1 -> x2, starting transfers between devices: 13.8 us -> 25.7 us  [the longest x1 13.6 us: on_device(): lax.all_to_all(outbox, 'request', split_axis=0, concat_axis=0, tiled=True)]
  transfers between devices with their start and end apart: 3 -> 20, of which waited for: 3 -> 10; matrix products, arithmetic and copies ran while one was open for 7% -> 18% of each run, Pallas kernels for 0% -> 0%
where the time goes in v1:
time: 321 us; the launch traced here: 318 us
  waiting for transfers between devices  189 us (59%)
  matrix products  52.5 us (16%)
  starting transfers between devices  35.7 us (11%)
  local copies, waits for them, and re-layouts  23.9 us (7%)
  other arithmetic  14.8 us (5%)
    ppermute x18, waiting for transfers between devices, flip(): return lax.ppermute(value, 'tensor', [(i, i ^ mask) for i in range(groups)])  142 us
    all_to_all x1, waiting for transfers between devices, on_device(): lax.all_to_all(expert_out, 'request', split_axis=0, concat_axis=0, tiled=...  47.6 us
    dot_general x4, matrix products, on_device(): total = total + jnp.dot(act, down_w, preferred_element_type=jnp.float32)  28 us
    all_to_all x1, starting transfers between devices, on_device(): lax.all_to_all(outbox, 'request', split_axis=0, concat_axis=0, tiled=True)  13.6 us
    dot_general x4, matrix products, on_device(): gate = jnp.dot(inbox, gate_w, preferred_element_type=jnp.float32)  12.7 us
    all_to_all x1, starting transfers between devices, on_device(): lax.all_to_all(expert_out, 'request', split_axis=0, concat_axis=0, tiled=...  12.1 us
    ppermute x18, starting transfers between devices, flip(): return lax.ppermute(value, 'tensor', [(i, i ^ mask) for i in range(groups)])  10 us
    dynamic_update_slice x4, local copies, waits for them, and re-layouts, on_device(): decode = lax.dynamic_update_slice_in_dim(decode, piece, peer * quarter, 2)  6.58 us
  transfers between devices with their start and end apart: 20, of which 10 were waited for; matrix products, arithmetic and copies ran while one was open for 18% of the time, Pallas kernels for 0%

profile of v1, /device:TPU:32, one launch (start us, length us, event | category | flops | bytes accessed | tf_op | source)
XLA Modules:
  0.0 318.0 jit_solution(10304707723878277047)
XLA Ops:
  6.7 2.3 copy.46
  12.5 2.1 fusion.69
  15.2 2.4 fusion.70
  17.6 2.9 collective-permute-done
  22.2 1.9 collective-permute-start.1
  24.2 12.2 %collective-permute-done.1 = bf16[256,1024]{1,0:T(8,128)(2,1)S(1)} collective-permute-done((bf16[256,1024]{1,0:T(8,128)(2,1)S(1)}, bf16[256,1024]{1,0:T(8,128)(2,1)S(1)}, u32[]{:S(2)}, u32[]{:S(2)}) %collective-permute-start.1) | collective-permute-done | bytes 524320 | tf_op jit(solution)/shard_map/ppermute | solution.py:47
  41.3 2.2 fusion.2
  43.5 13.6 %all-to-all-start = ((bf16[64,8,2048]{2,1,0:T(8,128)(2,1)}), bf16[64,8,2048]{2,1,0:T(8,128)(2,1)S(1)}, u32[]{:S(2)}, u32[]{:S(2)}) async-start(bf16[64,8,2048]{2,1,0:T(8,128)(2,1)} %fusion.2), calls=%async_computation | async-start | bytes 4194304 | tf_op jit(solution)/shard_map/all_to_all | solution.py:123
  60.8 3.1 select_bitcast_fusion.1
  63.8 2.8 dynamic_update_slice.24
  66.6 2.8 dynamic_update_slice.25
  69.4 3.0 pad_maximum_fusion
  72.5 63.3 %collective-permute-done.6 = bf16[2048,352]{0,1:T(8,128)(2,1)} collective-permute-done((bf16[2048,352]{0,1:T(8,128)(2,1)}, bf16[2048,352]{0,1:T(8,128)(2,1)}, u32[]{:S(2)}, u32[]{:S(2)}) %collective-permute-start.6) | collective-permute-done | bytes 1441824 | tf_op jit(solution)/shard_map/ppermute | solution.py:47
  135.7 3.2 fusion.58
  138.9 6.2 %fusion.14 = f32[512,2048]{1,0:T(8,128)} fusion(bf16[512,2048]{1,0:T(8,128)(2,1)S(1)} %bitcast.93, f32[512,352]{0,1:T(8,128)} %fusion.58, bf16[1,352,2048]{2,1,0:T(8,128)(2,1)} %param.27, bf16[1,2048,352]{1,2,0:T(8,128)(2,1)} %param.26), kind=kOutput, calls=%fused_computation.28 | convolution fusion | flops 1477476352 | bytes 9895936 | tf_op jit(solution)/shard_map/dot_general | solution.py:136
  145.6 3.2 fusion.78
  148.7 17.9 %collective-permute-done.7 = bf16[2048,352]{0,1:T(8,128)(2,1)} collective-permute-done((bf16[2048,352]{0,1:T(8,128)(2,1)}, bf16[2048,352]{0,1:T(8,128)(2,1)}, u32[]{:S(2)}, u32[]{:S(2)}) %collective-permute-start.7) | collective-permute-done | bytes 1441824 | tf_op jit(solution)/shard_map/ppermute | solution.py:47
  166.6 30.1 %collective-permute-done.8 = bf16[352,2048]{1,0:T(8,128)(2,1)} collective-permute-done((bf16[352,2048]{1,0:T(8,128)(2,1)}, bf16[352,2048]{1,0:T(8,128)(2,1)}, u32[]{:S(2)}, u32[]{:S(2)}) %collective-permute-start.8) | collective-permute-done | bytes 1441824 | tf_op jit(solution)/shard_map/ppermute | solution.py:47
  196.7 3.2 %fusion.77 = f32[512,352]{0,1:T(8,128)} fusion(bf16[512,2048]{1,0:T(8,128)(2,1)S(1)} %bitcast.95, bf16[2048,352]{0,1:T(8,128)(2,1)} %collective-permute-done.3), kind=kOutput, calls=%fused_computation.120 | convolution fusion | flops 738197504 | bytes 4259840 | tf_op jit(solution)/shard_map/dot_general | solution.py:133
  199.9 3.2 fusion.79
  203.1 6.2 %fusion.35 = f32[512,2048]{1,0:T(8,128)} fusion(bf16[352,2048]{1,0:T(8,128)(2,1)} %collective-permute-done.8, f32[512,352]{0,1:T(8,128)} %fusion.78, bf16[512,2048]{1,0:T(8,128)(2,1)S(1)} %bitcast.97, bf16[2048,352]{0,1:T(8,128)(2,1)} %collective-permute-done.7), kind=kOutput, calls=%fused_computation.71 | convolution fusion | flops 1477476352 | bytes 9895936 | tf_op jit(solution)/shard_map/dot_general | solution.py:136
  209.3 6.2 %fusion.34 = f32[512,2048]{1,0:T(8,128)} fusion(bf16[352,2048]{1,0:T(8,128)(2,1)} %collective-permute-done.5, f32[512,352]{0,1:T(8,128)} %fusion.77, bf16[512,2048]{1,0:T(8,128)(2,1)S(1)} %bitcast.98, bf16[2048,352]{0,1:T(8,128)(2,1)} %collective-permute-done.4), kind=kOutput, calls=%fused_computation.70 | convolution fusion | flops 1477476352 | bytes 9895936 | tf_op jit(solution)/shard_map/dot_general | solution.py:136
  215.5 9.4 %fusion.3 = bf16[64,8,2048]{2,1,0:T(8,128)(2,1)} fusion(bf16[352,2048]{1,0:T(8,128)(2,1)} %collective-permute-done.11, f32[512,2048]{1,0:T(8,128)} %fusion.35, f32[512,2048]{1,0:T(8,128)} %fusion.14, f32[512,2048]{1,0:T(8,128)} %fusion.34, f32[512,352]{0,1:T(8,128)} %fusion.79, bf16[512,2048]{1,0:T(8,128)(2,1)S(1)} %bitcast.99, ...), kind=kOutput, calls=%fused_computation.8 | convolution fusion | flops 1481670656 | bytes 20381696 | tf_op jit(solution)/shard_map/dot_general | solution.py:136
  224.9 12.1 %all-to-all-start.1 = ((bf16[64,8,2048]{2,1,0:T(8,128)(2,1)}), bf16[64,8,2048]{2,1,0:T(8,128)(2,1)}, u32[]{:S(2)}, u32[]{:S(2)}) async-start(bf16[64,8,2048]{2,1,0:T(8,128)(2,1)} %fusion.3), calls=%async_computation.1 | async-start | bytes 4194304 | tf_op jit(solution)/shard_map/all_to_all | solution.py:148
  242.7 1.9 bitcast_dynamic-update-slice_fusion.2
  244.6 47.6 %all-to-all-done.1 = bf16[64,8,2048]{2,1,0:T(8,128)(2,1)} async-done(((bf16[64,8,2048]{2,1,0:T(8,128)(2,1)}), bf16[64,8,2048]{2,1,0:T(8,128)(2,1)}, u32[]{:S(2)}, u32[]{:S(2)}) %all-to-all-start.1) | async-done | bytes 2097184 | tf_op jit(solution)/shard_map/all_to_all | solution.py:148
  292.2 2.4 convolution_bitcast_fusion
  294.5 2.4 fusion.4
  299.0 2.0 bitcast_dynamic-update-slice_fusion.1
  301.0 4.9 %collective-permute-done.17 = bf16[2,256,512]{2,1,0:T(8,128)(2,1)} collective-permute-done((bf16[2,256,512]{2,1,0:T(8,128)(2,1)}, bf16[2,256,512]{2,1,0:T(8,128)(2,1)}, u32[]{:S(2)}, u32[]{:S(2)}) %collective-permute-start.17) | collective-permute-done | bytes 524320 | tf_op jit(solution)/shard_map/ppermute | solution.py:47
  307.8 4.6 %collective-permute-done.13 = bf16[256,512]{1,0:T(8,128)(2,1)S(1)} collective-permute-done((bf16[256,512]{1,0:T(8,128)(2,1)S(1)}, bf16[256,512]{1,0:T(8,128)(2,1)S(1)}, u32[]{:S(2)}, u32[]{:S(2)}) %collective-permute-start.13) | collective-permute-done | bytes 262176 | tf_op jit(solution)/shard_map/ppermute | solution.py:47
  312.4 4.7 %collective-permute-done.14 = bf16[256,512]{1,0:T(8,128)(2,1)S(1)} collective-permute-done((bf16[256,512]{1,0:T(8,128)(2,1)S(1)}, bf16[256,512]{1,0:T(8,128)(2,1)S(1)}, u32[]{:S(2)}, u32[]{:S(2)}) %collective-permute-start.14) | collective-permute-done | bytes 262176 | tf_op jit(solution)/shard_map/ppermute | solution.py:47
  (83 shorter events, 30.5 us)
Async XLA Ops:
  0.6 14.5 %copy-start = (bf16[512,2048]{1,0:T(8,128)(2,1)S(1)}, bf16[512,2048]{1,0:T(8,128)(2,1)}, u32[]{:S(2)}) copy-start(bf16[512,2048]{1,0:T(8,128)(2,1)} %param.21) | copy-start | bytes 6291460
  0.6 3.4 %copy-start.6 = (bf16[256,512]{1,0:T(8,128)(2,1)S(1)}, bf16[256,512]{1,0:T(8,128)(2,1)}, u32[]{:S(2)}) copy-start(bf16[256,512]{1,0:T(8,128)(2,1)} %param.16) | copy-start | bytes 786436
  2.9 6.1 %copy-start.7 = (bf16[256,512]{1,0:T(8,128)(2,1)S(1)}, bf16[256,512]{1,0:T(8,128)(2,1)}, u32[]{:S(2)}) copy-start(bf16[256,512]{1,0:T(8,128)(2,1)} %param.17) | copy-start | bytes 786436
  4.1 6.7 %copy-start.4 = (bf16[768,4,128]{2,0,1:T(8,128)(2,1)S(1)}, bf16[768,4,128]{2,0,1:T(8,128)(2,1)}, u32[]{:S(2)}) copy-start(bf16[768,4,128]{2,0,1:T(8,128)(2,1)} %copy.50) | copy-start | bytes 2359300
  12.5 2.2 copy-start.9
  12.5 2.2 copy-start.10
  17.6 18.8 %copy-start.3 = (f32[256,2048]{1,0:T(8,128)S(1)}, f32[256,2048]{1,0:T(8,128)}, u32[]{:S(2)}) copy-start(f32[256,2048]{1,0:T(8,128)} %get-tuple-element.21) | copy-start | bytes 6291460
  17.6 2.9 collective-permute-start
  20.5 3.7 %copy-start.8 = (bf16[256,2048]{1,0:T(8,128)(2,1)}, bf16[256,2048]{1,0:T(8,128)(2,1)S(1)}, u32[]{:S(2)}) copy-start(bf16[256,2048]{1,0:T(8,128)(2,1)S(1)} %collective-permute-done) | copy-start | bytes 3145732
  22.2 15.9 %copy-start.11 = (s32[256,4]{0,1:T(4,128)S(1)}, s32[256,4]{0,1:T(4,128)}, u32[]{:S(2)}) copy-start(s32[256,4]{0,1:T(4,128)} %param.23) | copy-start | bytes 12292
  22.2 14.1 %collective-permute-start.1 = (bf16[256,1024]{1,0:T(8,128)(2,1)S(1)}, bf16[256,1024]{1,0:T(8,128)(2,1)S(1)}, u32[]{:S(2)}, u32[]{:S(2)}) collective-permute-start(bf16[256,1024]{1,0:T(8,128)(2,1)S(1)} %fusion.33), channel_id=1, source_target_pairs={{0,128},{64,192},{128,0},{192,64},{1,129},{65,193},{129,1},{193,65... | collective-permute-start | bytes 1572872 | tf_op jit(solution)/shard_map/ppermute | solution.py:47
  37.9 3.4 %copy-start.13 = (f32[2048]{0:T(1024)S(1)}, f32[2048]{0:T(1024)}, u32[]{:S(2)}) copy-start(f32[2048]{0:T(1024)} %param.22) | copy-start | bytes 24580
  37.9 2.0 collective-permute-start.2
  43.5 92.2 %all-to-all-start = ((bf16[64,8,2048]{2,1,0:T(8,128)(2,1)}), bf16[64,8,2048]{2,1,0:T(8,128)(2,1)S(1)}, u32[]{:S(2)}, u32[]{:S(2)}) async-start(bf16[64,8,2048]{2,1,0:T(8,128)(2,1)} %fusion.2), calls=%async_computation | async-start | bytes 4194304 | tf_op jit(solution)/shard_map/all_to_all | solution.py:123
  57.1 78.6 %collective-permute-start.6 = (bf16[2048,352]{0,1:T(8,128)(2,1)}, bf16[2048,352]{0,1:T(8,128)(2,1)}, u32[]{:S(2)}, u32[]{:S(2)}) collective-permute-start(bf16[2048,352]{0,1:T(8,128)(2,1)} %bitcast.109), channel_id=1, source_target_pairs={{0,128},{64,192},{128,0},{192,64},{1,129},{65,193},{129,1},{193,65... | collective-permute-start | bytes 4325384 | tf_op jit(solution)/shard_map/ppermute | solution.py:47
  58.2 86.9 %collective-permute-start.3 = (bf16[2048,352]{0,1:T(8,128)(2,1)}, bf16[2048,352]{0,1:T(8,128)(2,1)}, u32[]{:S(2)}, u32[]{:S(2)}) collective-permute-start(bf16[2048,352]{0,1:T(8,128)(2,1)} %bitcast.110), channel_id=1, source_target_pairs={{0,64},{64,0},{128,192},{192,128},{1,65},{65,1},{129,193},{193,129... | collective-permute-start | bytes 4325384 | tf_op jit(solution)/shard_map/ppermute | solution.py:47
  58.2 151.1 %collective-permute-start.4 = (bf16[2048,352]{0,1:T(8,128)(2,1)}, bf16[2048,352]{0,1:T(8,128)(2,1)}, u32[]{:S(2)}, u32[]{:S(2)}) collective-permute-start(bf16[2048,352]{0,1:T(8,128)(2,1)} %bitcast.111), channel_id=1, source_target_pairs={{0,64},{64,0},{128,192},{192,128},{1,65},{65,1},{129,193},{193,129... | collective-permute-start | bytes 4325384 | tf_op jit(solution)/shard_map/ppermute | solution.py:47
  58.7 107.9 %collective-permute-start.7 = (bf16[2048,352]{0,1:T(8,128)(2,1)}, bf16[2048,352]{0,1:T(8,128)(2,1)}, u32[]{:S(2)}, u32[]{:S(2)}) collective-permute-start(bf16[2048,352]{0,1:T(8,128)(2,1)} %bitcast.112), channel_id=1, source_target_pairs={{0,128},{64,192},{128,0},{192,64},{1,129},{65,193},{129,1},{193,65... | collective-permute-start | bytes 4325384 | tf_op jit(solution)/shard_map/ppermute | solution.py:47
  59.7 136.9 %collective-permute-start.8 = (bf16[352,2048]{1,0:T(8,128)(2,1)}, bf16[352,2048]{1,0:T(8,128)(2,1)}, u32[]{:S(2)}, u32[]{:S(2)}) collective-permute-start(bf16[352,2048]{1,0:T(8,128)(2,1)} %bitcast.113), channel_id=1, source_target_pairs={{0,128},{64,192},{128,0},{192,64},{1,129},{65,193},{129,1},{193,65... | collective-permute-start | bytes 4325384 | tf_op jit(solution)/shard_map/ppermute | solution.py:47
  135.7 64.2 %collective-permute-start.9 = (bf16[2048,352]{0,1:T(8,128)(2,1)}, bf16[2048,352]{0,1:T(8,128)(2,1)}, u32[]{:S(2)}, u32[]{:S(2)}) collective-permute-start(bf16[2048,352]{0,1:T(8,128)(2,1)} %collective-permute-done.6), channel_id=1, source_target_pairs={{0,64},{64,0},{128,192},{192,128},{1,65},{65,1},{129,193},{193,129... | collective-permute-start | bytes 4325384 | tf_op jit(solution)/shard_map/ppermute | solution.py:47
  145.1 64.2 %collective-permute-start.5 = (bf16[352,2048]{1,0:T(8,128)(2,1)}, bf16[352,2048]{1,0:T(8,128)(2,1)}, u32[]{:S(2)}, u32[]{:S(2)}) collective-permute-start(bf16[352,2048]{1,0:T(8,128)(2,1)} %bitcast.114), channel_id=1, source_target_pairs={{0,64},{64,0},{128,192},{192,128},{1,65},{65,1},{129,193},{193,129... | collective-permute-start | bytes 4325384 | tf_op jit(solution)/shard_map/ppermute | solution.py:47
  166.6 48.9 %collective-permute-start.10 = (bf16[2048,352]{0,1:T(8,128)(2,1)}, bf16[2048,352]{0,1:T(8,128)(2,1)}, u32[]{:S(2)}, u32[]{:S(2)}) collective-permute-start(bf16[2048,352]{0,1:T(8,128)(2,1)} %collective-permute-done.7), channel_id=1, source_target_pairs={{0,64},{64,0},{128,192},{192,128},{1,65},{65,1},{129,193},{193,129... | collective-permute-start | bytes 4325384 | tf_op jit(solution)/shard_map/ppermute | solution.py:47
  196.7 18.9 %collective-permute-start.11 = (bf16[352,2048]{1,0:T(8,128)(2,1)}, bf16[352,2048]{1,0:T(8,128)(2,1)}, u32[]{:S(2)}, u32[]{:S(2)}) collective-permute-start(bf16[352,2048]{1,0:T(8,128)(2,1)} %collective-permute-done.8), channel_id=1, source_target_pairs={{0,64},{64,0},{128,192},{192,128},{1,65},{65,1},{129,193},{193,129... | collective-permute-start | bytes 4325384 | tf_op jit(solution)/shard_map/ppermute | solution.py:47
  224.9 12.2 %copy-start.2 = (bf16[2,1024,512]{2,1,0:T(8,128)(2,1)S(1)}, bf16[2,1024,512]{2,1,0:T(8,128)(2,1)}, u32[]{:S(2)}) copy-start(bf16[2,1024,512]{2,1,0:T(8,128)(2,1)} %pad_maximum_fusion) | copy-start | bytes 6291460
  224.9 67.2 %all-to-all-start.1 = ((bf16[64,8,2048]{2,1,0:T(8,128)(2,1)}), bf16[64,8,2048]{2,1,0:T(8,128)(2,1)}, u32[]{:S(2)}, u32[]{:S(2)}) async-start(bf16[64,8,2048]{2,1,0:T(8,128)(2,1)} %fusion.3), calls=%async_computation.1 | async-start | bytes 4194304 | tf_op jit(solution)/shard_map/all_to_all | solution.py:148
  238.3 4.4 %collective-permute-start.15 = (bf16[2,256,512]{2,1,0:T(8,128)(2,1)}, bf16[2,256,512]{2,1,0:T(8,128)(2,1)}, u32[]{:S(2)}, u32[]{:S(2)}) collective-permute-start(bf16[2,256,512]{2,1,0:T(8,128)(2,1)} %get-tuple-element.8), channel_id=1, source_target_pairs={{0,64},{64,0},{128,192},{192,128},{1,65},{65,1},{129,193},{193,129... | collective-permute-start | bytes 1572872 | tf_op jit(solution)/shard_map/ppermute | solution.py:47
  238.6 60.4 %collective-permute-start.16 = (bf16[2,256,512]{2,1,0:T(8,128)(2,1)}, bf16[2,256,512]{2,1,0:T(8,128)(2,1)}, u32[]{:S(2)}, u32[]{:S(2)}) collective-permute-start(bf16[2,256,512]{2,1,0:T(8,128)(2,1)} %get-tuple-element.7), channel_id=1, source_target_pairs={{0,128},{64,192},{128,0},{192,64},{1,129},{65,193},{129,1},{193,65... | collective-permute-start | bytes 1572872 | tf_op jit(solution)/shard_map/ppermute | solution.py:47
  239.7 66.2 %collective-permute-start.17 = (bf16[2,256,512]{2,1,0:T(8,128)(2,1)}, bf16[2,256,512]{2,1,0:T(8,128)(2,1)}, u32[]{:S(2)}, u32[]{:S(2)}) collective-permute-start(bf16[2,256,512]{2,1,0:T(8,128)(2,1)} %get-tuple-element.6), channel_id=1, source_target_pairs={{0,192},{64,128},{128,64},{192,0},{1,193},{65,129},{129,65},{193,1... | collective-permute-start | bytes 1572872 | tf_op jit(solution)/shard_map/ppermute | solution.py:47
  297.0 10.8 %collective-permute-start.12 = (bf16[256,512]{1,0:T(8,128)(2,1)S(1)}, bf16[256,512]{1,0:T(8,128)(2,1)S(1)}, u32[]{:S(2)}, u32[]{:S(2)}) collective-permute-start(bf16[256,512]{1,0:T(8,128)(2,1)S(1)} %get-tuple-element.9), channel_id=1, source_target_pairs={{0,64},{64,0},{128,192},{192,128},{1,65},{65,1},{129,193},{193,129... | collective-permute-start | bytes 786440 | tf_op jit(solution)/shard_map/ppermute | solution.py:47
  297.1 15.2 %collective-permute-start.13 = (bf16[256,512]{1,0:T(8,128)(2,1)S(1)}, bf16[256,512]{1,0:T(8,128)(2,1)S(1)}, u32[]{:S(2)}, u32[]{:S(2)}) collective-permute-start(bf16[256,512]{1,0:T(8,128)(2,1)S(1)} %get-tuple-element.11), channel_id=1, source_target_pairs={{0,128},{64,192},{128,0},{192,64},{1,129},{65,193},{129,1},{193,65... | collective-permute-start | bytes 786440 | tf_op jit(solution)/shard_map/ppermute | solution.py:47
  298.3 18.7 %collective-permute-start.14 = (bf16[256,512]{1,0:T(8,128)(2,1)S(1)}, bf16[256,512]{1,0:T(8,128)(2,1)S(1)}, u32[]{:S(2)}, u32[]{:S(2)}) collective-permute-start(bf16[256,512]{1,0:T(8,128)(2,1)S(1)} %get-tuple-element.10), channel_id=1, source_target_pairs={{0,192},{64,128},{128,64},{192,0},{1,193},{65,129},{129,65},{193,1... | collective-permute-start | bytes 786440 | tf_op jit(solution)/shard_map/ppermute | solution.py:47
  299.0 19.0 %copy-start.1 = (bf16[512,2048]{1,0:T(8,128)(2,1)S(1)}, bf16[512,2048]{1,0:T(8,128)(2,1)}, u32[]{:S(2)}) copy-start(bf16[512,2048]{1,0:T(8,128)(2,1)} %param.21) | copy-start | bytes 6291460
  (2 other events, 2.3 us)
